TPU v7x, 32 devices: a whole 2x2x4 slice. The times are simulated.
32 devices in a mesh: dp: 2 (over x), row: 4 (over z), col: 4 (over y, core).
Axes of the slice: x: 2, y: 2, z: 4, core: 2. Of those that a mesh axis runs over, the one named last changes fastest.
Arguments:
- block_input: bfloat16 [1024, 1024], P(('dp', 'col'), 'row'), may hold values from -6 to 6
- attn_gain: float32 [1024], P('row'), may hold values from 0.5 to 1.5
- query_weight: bfloat16 [1024, 1024], P('row', 'col'), may hold values from -0.1875 to 0.1875
- key_weight: bfloat16 [1024, 1024], P('row', 'col'), may hold values from -0.1875 to 0.1875
- value_weight: bfloat16 [1024, 2048], P('row', 'col'), may hold values from -0.1875 to 0.1875
- gate_weight: bfloat16 [1024, 2048], P('row', 'col'), may hold values from -0.1875 to 0.1875
- decay_weight: bfloat16 [1024, 8], P('row', 'col'), may hold values from -0.1875 to 0.1875
- beta_weight: bfloat16 [1024, 8], P('row', 'col'), may hold values from -0.1875 to 0.1875
- query_conv: float32 [4, 1024], P(None, 'col'), may hold values from -3 to 3
- key_conv: float32 [4, 1024], P(None, 'col'), may hold values from -3 to 3
- value_conv: float32 [4, 2048], P(None, 'col'), may hold values from -3 to 3
- decay_log: float32 [8], P('col'), may hold values from -4 to 0.5
- decay_bias: float32 [8], P('col'), may hold values from -3 to 0
- head_gain: float32 [256], replicated, may hold values from 0.5 to 1.5
- out_weight: bfloat16 [2048, 1024], P('col', 'row'), may hold values from -0.1875 to 0.1875
- ffn_gain: float32 [1024], P('row'), may hold values from 0.5 to 1.5
- ffn_gate: bfloat16 [1024, 2816], P('row', 'col'), may hold values from -0.1875 to 0.1875
- ffn_up: bfloat16 [1024, 2816], P('row', 'col'), may hold values from -0.1875 to 0.1875
- ffn_down: bfloat16 [2816, 1024], P('col', 'row'), may hold values from -0.15625 to 0.15625
- out_grad: bfloat16 [1024, 1024], P(('dp', 'col'), 'row'), may hold values from -6 to 6
- seq_starts: int32 [8, 1], replicated, may hold values from 0 to 64, as said below
- seq_lengths: int32 [8, 1], replicated, may hold values from 1 to 128, as said below
Outputs:
- output: bfloat16 [1024, 1024], P(('dp', 'col'), 'row')
- input_grad: float32 [1024, 1024], P(('dp', 'col'), 'row')
- attn_gain_grad: float32 [1024], P('row')
- query_weight_grad: float32 [1024, 1024], P('row', 'col')
- key_weight_grad: float32 [1024, 1024], P('row', 'col')
- value_weight_grad: float32 [1024, 2048], P('row', 'col')
- gate_weight_grad: float32 [1024, 2048], P('row', 'col')
- decay_weight_grad: float32 [1024, 8], P('row', 'col')
- beta_weight_grad: float32 [1024, 8], P('row', 'col')
- query_conv_grad: float32 [4, 1024], P(None, 'col')
- key_conv_grad: float32 [4, 1024], P(None, 'col')
- value_conv_grad: float32 [4, 2048], P(None, 'col')
- decay_log_grad: float32 [8], P('col')
- decay_bias_grad: float32 [8], P('col')
- head_gain_grad: float32 [256], replicated
- out_weight_grad: float32 [2048, 1024], P('col', 'row')
- ffn_gain_grad: float32 [1024], P('row')
- ffn_gate_grad: float32 [1024, 2816], P('row', 'col')
- ffn_up_grad: float32 [1024, 2816], P('row', 'col')
- ffn_down_grad: float32 [2816, 1024], P('col', 'row')
Inputs may be any that keep to these rules, and one draw needn't show every extreme that they name: `seq_starts`: sequences of a slot are in order and do not intersect; sequence i starts within tokens i * 128 to i * 128 + 128 // 2 of its slot and ends by (i + 1) * 128 - 1; in every draw some sequence starts at the last of these in the slot's last region. `seq_lengths`: in every draw some sequence is 128 tokens long.
All inputs are finite; a program needn't handle non-finite values.
Results may differ from a plain program's by a relative error of at most 0.012.
Values may be sent and summed in bfloat16 or wider, within the bound.
A program may use at most 128 MiB of HBM per device.

v0:
```python
import jax
import jax.numpy as jnp
from jax import lax
from jax.sharding import PartitionSpec as P

BLOCK = 64


epsilon = 1e-06
highest = lax.Precision.HIGHEST


def segment_info(starts, lengths, count):
    position = jnp.arange(count, dtype=jnp.int32)[:, None]
    begun = (position >= starts[None, :]).astype(jnp.int32)
    ended = (position >= (starts + lengths)[None, :]).astype(jnp.int32)
    segment = jnp.sum(begun + ended, axis=1)
    inside = jnp.sum(begun - ended, axis=1).astype(jnp.float32)
    return (segment, inside)


def short_conv(signal, kernel, segment):
    length = signal.shape[0]
    tap_count = kernel.shape[0]
    running_total = kernel[tap_count - 1] * signal
    for offset in range(1, tap_count):
        moved = jnp.pad(signal, ((offset, 0), (0, 0)))[:length]
        earlier = jnp.pad(segment, (offset, 0), constant_values=-1)[:length]
        running_total = running_total + kernel[tap_count - 1 - offset] * jnp.where(
            (earlier == segment)[:, None], moved, 0.0
        )
    return jax.nn.silu(running_total)


def unit_heads(signal, head_count):
    shaped = signal.reshape(signal.shape[0], head_count, -1)
    return shaped * lax.rsqrt(jnp.sum(shaped * shaped, axis=-1, keepdims=True) + epsilon)


def delta_rule(queries, key_heads, value_heads, write_rate, log_decay, segment):
    length, head_count, key_size = queries.shape
    value_size = value_heads.shape[2]
    blocks = length // BLOCK
    position = jnp.arange(BLOCK, dtype=jnp.int32)
    later_mask = position[:, None] > position[None, :]
    upto_mask = position[:, None] >= position[None, :]

    def advance(carry, pieces):
        memory, last_segment = carry
        block_query, block_key, block_value, block_rate, block_decay, block_segment = pieces
        cumulative = jnp.cumsum(block_decay, axis=0)
        same_segment = block_segment[:, None] == block_segment[None, :]
        strict = (same_segment & later_mask).astype(jnp.float32)
        within = (same_segment & upto_mask).astype(jnp.float32)
        carried = (block_segment == last_segment).astype(jnp.float32)
        decay_ratio = jnp.exp(jnp.minimum(cumulative.T[:, :, None] - cumulative.T[:, None, :], 0.0))
        key_dots = jnp.einsum("thd,jhd->htj", block_key, block_key, precision=highest)
        query_dots = jnp.einsum("thd,jhd->htj", block_query, block_key, precision=highest)
        lower_part = block_rate.T[:, :, None] * decay_ratio * key_dots * strict
        decayed = (jnp.exp(cumulative) * carried[:, None]).T
        recalled = jnp.einsum("hvk,thk->htv", memory, block_key, precision=highest)
        target = block_rate.T[:, :, None] * (
            jnp.transpose(block_value, (1, 0, 2)) - decayed[:, :, None] * recalled
        )
        writes = jax.scipy.linalg.solve_triangular(
            lower_part, target, lower=True, unit_diagonal=True
        )
        readout = decayed[:, :, None] * jnp.einsum(
            "hvk,thk->htv", memory, block_query, precision=highest
        )
        readout = readout + jnp.einsum(
            "htj,hjv->htv", decay_ratio * query_dots * within, writes, precision=highest
        )
        closing = (block_segment == block_segment[-1]).astype(jnp.float32)
        ending = jnp.exp(cumulative[-1][None, :] - cumulative) * closing[:, None]
        memory = memory * decayed[:, -1][:, None, None] + jnp.einsum(
            "jh,hjv,jhk->hvk", ending, writes, block_key, precision=highest
        )
        return ((memory, block_segment[-1]), jnp.transpose(readout, (1, 0, 2)))

    def blocked(array):
        return array.reshape((blocks, BLOCK) + array.shape[1:])

    initial = (jnp.zeros((head_count, value_size, key_size), jnp.float32), jnp.array(-1, jnp.int32))
    final_carry, stacked = lax.scan(
        advance,
        initial,
        (
            blocked(queries),
            blocked(key_heads),
            blocked(value_heads),
            blocked(write_rate),
            blocked(log_decay),
            blocked(segment),
        ),
    )
    return stacked.reshape(length, head_count, value_size)


def token_mixer(linears, params, segment, inside):
    query_lin, key_lin, value_lin, gate_lin, decay_lin, rate_lin = linears
    conv_query, conv_key, conv_value, log_rate, rate_bias, norm_gain = params
    head_count = log_rate.shape[0]
    length = query_lin.shape[0]
    queries = unit_heads(short_conv(query_lin, conv_query, segment), head_count)
    queries = queries * queries.shape[-1] ** (-0.5)
    key_heads = unit_heads(short_conv(key_lin, conv_key, segment), head_count)
    value_heads = short_conv(value_lin, conv_value, segment).reshape(length, head_count, -1)
    write_rate = jax.nn.sigmoid(rate_lin)
    log_decay = -jnp.exp(log_rate) * jax.nn.softplus(decay_lin + rate_bias)
    mixed_heads = delta_rule(queries, key_heads, value_heads, write_rate, log_decay, segment)
    normed = (
        mixed_heads
        * lax.rsqrt(jnp.mean(mixed_heads * mixed_heads, axis=-1, keepdims=True) + epsilon)
        * norm_gain
    )
    gate_heads = jax.nn.silu(gate_lin.reshape(length, head_count, -1))
    return (normed * gate_heads * inside[:, None, None]).reshape(length, -1)


def feature_total(values):
    return lax.psum(values, "row")


def norm_scale(values):
    feature_count = values.shape[1] * lax.axis_size("row")
    return lax.rsqrt(feature_total(jnp.sum(values * values, axis=1)) / feature_count + epsilon)


def norm_backward(values, row_scale, gain_vector, upstream):
    feature_count = values.shape[1] * lax.axis_size("row")
    weighted = upstream * gain_vector
    inner_mean = feature_total(jnp.sum(weighted * values, axis=1)) / feature_count
    grad_values = (
        row_scale[:, None] * weighted
        - values * (row_scale * row_scale * row_scale * inner_mean)[:, None]
    )
    return (grad_values, jnp.sum(upstream * values * row_scale[:, None], axis=0))


def token_gather(values):
    return lax.all_gather(values, "col", axis=0, tiled=True)


def head_gather(values):
    return lax.all_gather(values, "row", axis=0, tiled=True)


def product_terms(left, right, flipped):
    inner_dim = 1 if flipped else 0
    return lax.dot_general(
        left, right, (((1,), (inner_dim,)), ((), ())), preferred_element_type=jnp.float32
    )


def head_sums(left, right, flipped):
    return lax.psum_scatter(
        product_terms(left, right, flipped), "row", scatter_dimension=0, tiled=True
    )


def token_sums(left, right, flipped):
    return lax.psum_scatter(
        product_terms(left, right, flipped), "col", scatter_dimension=0, tiled=True
    )


def weight_grad(left, right):
    return lax.dot_general(
        left, right, (((0,), (0,)), ((), ())), preferred_element_type=jnp.float32
    )


def split_points(matrices):
    edges = []
    running_total = 0
    for matrix in matrices[:-1]:
        running_total = running_total + matrix.shape[1]
        edges.append(running_total)
    return edges


def shards(
    block_input,
    attn_gain,
    query_weight,
    key_weight,
    value_weight,
    gate_weight,
    decay_weight,
    beta_weight,
    query_conv,
    key_conv,
    value_conv,
    decay_log,
    decay_bias,
    head_gain,
    out_weight,
    ffn_gain,
    ffn_gate,
    ffn_up,
    ffn_down,
    out_grad,
    seq_starts,
    seq_lengths,
):
    slot_rows = block_input.shape[0]
    slot_index = lax.axis_index("dp") * lax.axis_size("col") + lax.axis_index("row")
    starts = lax.dynamic_index_in_dim(seq_starts, slot_index, 0, keepdims=False)
    lengths = lax.dynamic_index_in_dim(seq_lengths, slot_index, 0, keepdims=False)
    segment, inside = segment_info(starts, lengths, slot_rows)
    inputs = block_input.astype(jnp.float32)
    first_scale = norm_scale(inputs)
    first_normalized = (inputs * first_scale[:, None] * attn_gain).astype(jnp.bfloat16)
    gathered_first = token_gather(first_normalized)
    in_list = (query_weight, key_weight, value_weight, gate_weight, decay_weight, beta_weight)
    in_edges = split_points(in_list)
    in_weights = jnp.concatenate(in_list, axis=1)
    projected = head_sums(gathered_first, in_weights, False)
    linears = tuple(jnp.split(projected, in_edges, axis=1))
    mixer_params = (query_conv, key_conv, value_conv, decay_log, decay_bias, head_gain)

    def mixer_piece(linear_set, param_set):
        return token_mixer(linear_set, param_set, segment, inside)

    gated, mixer_back = jax.vjp(mixer_piece, linears, mixer_params)
    mixer_output = gated.astype(jnp.bfloat16)
    mixed_rows = head_gather(mixer_output)
    resid = inputs + token_sums(mixed_rows, out_weight, False)
    second_scale = norm_scale(resid)
    second_normalized = (resid * second_scale[:, None] * ffn_gain).astype(jnp.bfloat16)
    gathered_second = token_gather(second_normalized)
    ffn_weights = jnp.concatenate([ffn_gate, ffn_up], axis=1)
    hidden_width = ffn_gate.shape[1]
    ffn_inner = head_sums(gathered_second, ffn_weights, False)
    gate_part = ffn_inner[:, :hidden_width]
    up_part = ffn_inner[:, hidden_width:]
    hidden_activation = (jax.nn.silu(gate_part) * up_part * inside[:, None]).astype(jnp.bfloat16)
    hidden_rows = head_gather(hidden_activation)
    output = (resid + token_sums(hidden_rows, ffn_down, False)).astype(jnp.bfloat16)
    grad_rows = token_gather(out_grad)
    down_grad = weight_grad(hidden_rows, grad_rows)
    grad_hidden = head_sums(grad_rows, ffn_down, True) * inside[:, None]
    sigmoid_gate = jax.nn.sigmoid(gate_part)
    gate_gradient = grad_hidden * up_part * sigmoid_gate * (1.0 + gate_part * (1.0 - sigmoid_gate))
    up_gradient = grad_hidden * gate_part * sigmoid_gate
    grad_ffn = jnp.concatenate([gate_gradient, up_gradient], axis=1).astype(jnp.bfloat16)
    grad_ffn_rows = head_gather(grad_ffn)
    ffn_weight_grad = weight_grad(gathered_second, grad_ffn_rows)
    gate_grad = ffn_weight_grad[:, :hidden_width]
    up_grad = ffn_weight_grad[:, hidden_width:]
    grad_second = token_sums(grad_ffn_rows, ffn_weights, True)
    resid_part, feedforward_gain_share = norm_backward(resid, second_scale, ffn_gain, grad_second)
    grad_resid = out_grad.astype(jnp.float32) + resid_part
    residual_signal_path = grad_resid.astype(jnp.bfloat16)
    resid_rows = token_gather(residual_signal_path)
    out_weight_grad = weight_grad(mixed_rows, resid_rows)
    grad_mixed = head_sums(resid_rows, out_weight, True)
    grad_linears, parameter_gradients = mixer_back(grad_mixed)
    linear_signal_path = jnp.concatenate(grad_linears, axis=1).astype(jnp.bfloat16)
    lin_rows = head_gather(linear_signal_path)
    in_weight_grad = weight_grad(gathered_first, lin_rows)
    in_grads = jnp.split(in_weight_grad, in_edges, axis=1)
    grad_first = token_sums(lin_rows, in_weights, True)
    input_part, attention_gain_share = norm_backward(inputs, first_scale, attn_gain, grad_first)
    input_grad = grad_resid + input_part
    param_sums = lax.psum(
        (
            parameter_gradients[0],
            parameter_gradients[1],
            parameter_gradients[2],
            parameter_gradients[3],
            parameter_gradients[4],
            parameter_gradients[5],
        ),
        "row",
    )
    gain_sums = lax.psum((attention_gain_share, feedforward_gain_share, param_sums[5]), "col")
    reduced_all = lax.psum(
        (
            gain_sums[0],
            in_grads[0],
            in_grads[1],
            in_grads[2],
            in_grads[3],
            in_grads[4],
            in_grads[5],
            param_sums[0],
            param_sums[1],
            param_sums[2],
            param_sums[3],
            param_sums[4],
            gain_sums[2],
            out_weight_grad,
            gain_sums[1],
            gate_grad,
            up_grad,
            down_grad,
        ),
        "dp",
    )
    reduced = reduced_all[:15]
    final_gate, final_up, final_down = (reduced_all[15], reduced_all[16], reduced_all[17])
    return (
        output,
        input_grad,
        reduced[0],
        reduced[1],
        reduced[2],
        reduced[3],
        reduced[4],
        reduced[5],
        reduced[6],
        reduced[7],
        reduced[8],
        reduced[9],
        reduced[10],
        reduced[11],
        reduced[12],
        reduced[13],
        reduced[14],
        final_gate,
        final_up,
        final_down,
    )


def solution(mesh):
    in_specs = (
        P(("dp", "col"), "row"),
        P("row"),
        P("row", "col"),
        P("row", "col"),
        P("row", "col"),
        P("row", "col"),
        P("row", "col"),
        P("row", "col"),
        P(None, "col"),
        P(None, "col"),
        P(None, "col"),
        P("col"),
        P("col"),
        P(),
        P("col", "row"),
        P("row"),
        P("row", "col"),
        P("row", "col"),
        P("col", "row"),
        P(("dp", "col"), "row"),
        P(),
        P(),
    )
    out_specs = (
        P(("dp", "col"), "row"),
        P(("dp", "col"), "row"),
        P("row"),
        P("row", "col"),
        P("row", "col"),
        P("row", "col"),
        P("row", "col"),
        P("row", "col"),
        P("row", "col"),
        P(None, "col"),
        P(None, "col"),
        P(None, "col"),
        P("col"),
        P("col"),
        P(),
        P("col", "row"),
        P("row"),
        P("row", "col"),
        P("row", "col"),
        P("col", "row"),
    )
    return jax.shard_map(shards, mesh=mesh, in_specs=in_specs, out_specs=out_specs, check_vma=False)
```

profile of v0, /device:TPU:0, one launch (start us, length us, event | category | flops | bytes accessed | tf_op | source)
XLA Modules:
  0.0 687.5 jit_solution(10647418359381445880)
XLA Ops:
  8.2 13.5 %psum.217 = f32[128]{0:T(128)S(1)} all-reduce(f32[128]{0:T(128)S(1)} %fusion.191), channel_id=1, replica_groups=mesh['dp'=2,'row'=4,'col'=4] {'row'}, use_global_device_ids=true, to_apply=%region_1.2 | all-reduce | flops 128 | bytes 1024 | tf_op jit(solution)/shard_map/psum | solution.py:122
  23.7 5.8 all_gather.24
  31.1 1.3 concatenate.14
  32.5 2.3 fusion.237
  36.0 1.2 fusion.236
  37.2 1.3 fusion.218
  38.5 1.8 subtract_convert_fusion.1
  40.4 1.9 fusion.212
  42.5 51.5 %reduce-scatter.9.cloned.1.call-done = f32[128,1540]{0,1:T(8,128)} async-done(((f32[512,1540]{0,1:T(8,128)}), f32[128,1540]{0,1:T(8,128)}) %reduce-scatter.9.cloned.1.call-update) | async-done | bytes 788496 | tf_op jit(solution)/shard_map/reduce_scatter | solution.py:157
  94.0 1.4 broadcast_multiply_fusion.3
  100.0 1.2 fusion.172
  102.4 44.5 %while.92 = (s32[]{:T(128)}, f32[2,256,128]{2,1,0:T(8,128)S(1)}, s32[]{:T(128)}, f32[2,64,2,256]{3,1,2,0:T(8,128)S(1)}, f32[2,2,64,64]{3,2,1,0:T(8,128)}, /*inde...) while((s32[]{:T(128)}, f32[2,256,128]{2,1,0:T(8,128)S(1)}, ...), condition=%wide.region_7.8_spmd.clone.clone, body=%wide.region_5.7_spmd.clone.clone.sunk | while | flops 227431616 | bytes 5051084 | solution.py:85
  103.5 1.2 constant_dynamic-update-slice_fusion.18
  108.2 9.8 %custom-call.51 = f32[2,1,64,64]{2,3,1,0:T(8,128)S(1)} custom-call(f32[2,1,64,64]{3,2,1,0:T(8,128)S(1)} %add_bitcast_fusion.5), custom_call_target="InvertDiagBlocksLowerTriangular" | custom-call | tf_op jit(solution)/shard_map/jvp()/while/body/eval_jaxpr/jit(_solve_triangular)/vmap()/triangular_solve | solution.py:65
  122.2 1.2 constant_dynamic-update-slice_fusion.21
  125.7 1.2 constant_dynamic-update-slice_fusion.18
  130.5 9.8 %custom-call.51 = f32[2,1,64,64]{2,3,1,0:T(8,128)S(1)} custom-call(f32[2,1,64,64]{3,2,1,0:T(8,128)S(1)} %add_bitcast_fusion.5), custom_call_target="InvertDiagBlocksLowerTriangular" | custom-call | tf_op jit(solution)/shard_map/jvp()/while/body/eval_jaxpr/jit(_solve_triangular)/vmap()/triangular_solve | solution.py:65
  147.7 1.7 fusion.231
  149.4 14.8 %all_gather.25 = bf16[512,512]{0,1:T(8,128)(2,1)S(1)} all-gather(bf16[128,512]{0,1:T(8,128)(2,1)S(1)} %get-tuple-element.2068), channel_id=1, replica_groups=mesh['dp'=2,'row'=4,'col'=4] {'row'}, dimensions={0}, use_global_device_ids=true | all-gather | bytes 655360 | tf_op jit(solution)/shard_map/all_gather | solution.py:146
  165.4 5.8 all_gather.28
  172.0 1.6 fusion.241
  175.6 10.1 %reduce-scatter.11.cloned.1.call-done = f32[128,256]{1,0:T(8,128)} async-done(((f32[512,256]{1,0:T(8,128)}), f32[128,256]{1,0:T(8,128)}) %reduce-scatter.11.cloned.1.call-update) | async-done | bytes 131088 | tf_op jit(solution)/shard_map/reduce_scatter | solution.py:163
  186.7 11.8 %psum.218 = f32[128]{0:T(128)S(1)} all-reduce(f32[128]{0:T(128)S(1)} %get-tuple-element.2001), channel_id=1, replica_groups=mesh['dp'=2,'row'=4,'col'=4] {'row'}, use_global_device_ids=true, to_apply=%region_11.12 | all-reduce | flops 128 | bytes 1024 | tf_op jit(solution)/shard_map/psum | solution.py:122
  198.6 5.8 all_gather.26
  205.1 2.2 fusion.239
  207.4 16.1 %reduce-scatter.17.cloned.1.call-done = f32[128,704]{1,0:T(8,128)} async-done(((f32[512,704]{1,0:T(8,128)}), f32[128,704]{1,0:T(8,128)}) %reduce-scatter.17.cloned.1.call-update) | async-done | bytes 360464 | tf_op jit(solution)/shard_map/reduce_scatter | solution.py:157
  223.5 57.3 %reduce-scatter.13.cloned.1.call-done = f32[128,1408]{1,0:T(8,128)} async-done(((f32[512,1408]{1,0:T(8,128)}), f32[128,1408]{1,0:T(8,128)}) %reduce-scatter.13.cloned.1.call-update) | async-done | bytes 720912 | tf_op jit(solution)/shard_map/reduce_scatter | solution.py:157
  280.9 2.2 multiply_convert_fusion.1
  284.0 34.6 %all-gather.3.cloned.1.call-done = bf16[512,1408]{1,0:T(8,128)(2,1)} async-done(((bf16[128,1408]{1,0:T(8,128)(2,1)}), bf16[512,1408]{1,0:T(8,128)(2,1)}) %all-gather.3.cloned.1.call-update) | async-done | bytes 1441808 | tf_op jit(solution)/shard_map/all_gather | solution.py:146
  318.6 2.7 fusion.242
  321.4 20.8 %reduce-scatter.19.cloned.1.call-done = f32[128,256]{1,0:T(8,128)} async-done(((f32[512,256]{1,0:T(8,128)}), f32[128,256]{1,0:T(8,128)}) %reduce-scatter.19.cloned.1.call-update) | async-done | bytes 131088 | tf_op jit(solution)/shard_map/reduce_scatter | solution.py:163
  342.2 1.6 multiply_reduce_fusion.7
  343.8 11.7 %psum.219 = f32[128]{0:T(128)S(1)} all-reduce(f32[128]{0:T(128)S(1)} %get-tuple-element.1813), channel_id=1, replica_groups=mesh['dp'=2,'row'=4,'col'=4] {'row'}, use_global_device_ids=true, to_apply=%region_17.18 | all-reduce | flops 128 | bytes 1024 | tf_op jit(solution)/shard_map/psum | solution.py:122
  356.6 6.1 all_gather.30
  363.4 1.4 fusion.243
  364.8 1.3 subtract_convert_fusion
  368.2 21.2 %reduce-scatter.21.cloned.1.call-done = f32[128,512]{0,1:T(8,128)} async-done(((f32[512,512]{0,1:T(8,128)}), f32[128,512]{0,1:T(8,128)}) %reduce-scatter.21.cloned.1.call-update) | async-done | bytes 262160 | tf_op jit(solution)/shard_map/reduce_scatter | solution.py:157
  391.4 2.8 multiply_reduce_fusion
  394.4 1.3 add_add_fusion
  399.0 52.2 %while.91 = (s32[]{:T(128)}, f32[2,256,128]{2,1,0:T(8,128)S(1)}, f32[2,64,2,128]{3,1,2,0:T(8,128)}, f32[2,64,2,128]{3,1,2,0:T(8,128)}, f32[2,64,2,256]{3,1,2,0:T...) while((s32[]{:T(128)}, f32[2,256,128]{2,1,0:T(8,128)S(1)}, ...), condition=%wide.region_30.31_spmd.clone, body=%wide.region_20.30_spmd.clone.sunk | while | flops 460772416 | bytes 14135957 | solution.py:85
  403.6 9.8 %custom-call.50 = f32[2,1,64,64]{2,3,1,0:T(8,128)S(1)} custom-call(f32[2,1,64,64]{3,2,1,0:T(8,128)S(1)} %add_bitcast_fusion.4), custom_call_target="InvertDiagBlocksLowerTriangular" | custom-call | tf_op jit(solution)/shard_map/transpose(jvp())/while/body/eval_jaxpr/jit(_solve_triangular)/vmap()/triangular_solve | solution.py:65
  416.8 1.2 bitcast_multiply_fusion.36
  420.9 1.3 dynamic_update_slice.263
  429.7 9.8 %custom-call.50 = f32[2,1,64,64]{2,3,1,0:T(8,128)S(1)} custom-call(f32[2,1,64,64]{3,2,1,0:T(8,128)S(1)} %add_bitcast_fusion.4), custom_call_target="InvertDiagBlocksLowerTriangular" | custom-call | tf_op jit(solution)/shard_map/transpose(jvp())/while/body/eval_jaxpr/jit(_solve_triangular)/vmap()/triangular_solve | solution.py:65
  442.9 1.2 bitcast_multiply_fusion.36
  447.0 1.3 dynamic_update_slice.263
  459.6 1.8 multiply_reduce_fusion.4
  462.7 2.2 multiply_reduce_fusion.8
  466.3 3.2 concatenate.17
  469.9 36.2 %all-gather.5.cloned.1.call-done = bf16[512,1540]{0,1:T(8,128)(2,1)} async-done(((bf16[128,1540]{0,1:T(8,128)(2,1)}), bf16[512,1540]{0,1:T(8,128)(2,1)}) %all-gather.5.cloned.1.call-update) | async-done | bytes 1576976 | tf_op jit(solution)/shard_map/all_gather | solution.py:146
  506.1 2.9 fusion.244
  509.1 17.9 %all_gather.27 = bf16[512,704]{1,0:T(8,128)(2,1)S(1)} all-gather(bf16[128,704]{1,0:T(8,128)(2,1)S(1)} %copy-done.54), channel_id=1, replica_groups=mesh['dp'=2,'row'=4,'col'=4] {'row'}, dimensions={0}, use_global_device_ids=true | all-gather | bytes 901120 | tf_op jit(solution)/shard_map/all_gather | solution.py:146
  527.0 1.2 fusion.240
  528.1 1.2 fusion.248
  529.5 1.5 fusion.247
  531.1 1.4 fusion.230
  538.0 17.4 %all-reduce.36 = (f32[128]{0:T(128)S(1)}, f32[256]{0:T(256)S(1)}, f32[4,256]{1,0:T(4,128)S(1)}, f32[4,256]{1,0:T(4,128)S(1)}, f32[4,512]{1,0:T(4,128)S(1)}, /*index=5*/f32[2]{0:T(128)S(1)}, f32[2]{0:T(128)S(1)}) all-reduce(f32[128]{0:T(128)S(1)} %get-tuple-element.1822, ...), channel_id=1, replica_groups=mesh['dp'=2,'row'=4,'col'=4] {'row'}, use_global_device_ids=true, to_apply=%region_35.36 | all-reduce | flops 4484 | bytes 35872 | tf_op jit(solution)/shard_map/psum | solution.py:122
  555.4 5.7 all-reduce.35
  561.0 10.0 %all-reduce.37 = (f32[256]{0:T(256)}, f32[256,2]{0,1:T(2,128)}, f32[256,2]{0,1:T(2,128)}, f32[4,256]{1,0:T(4,128)}, f32[4,256]{1,0:T(4,128)}, /*index=5*/f32[4,5...) all-reduce(f32[256]{0:T(256)S(1)} %get-tuple-element.1963, ...), channel_id=1, replica_groups=mesh['dp'=2,'row'=4,'col'=4] {'dp'}, use_global_device_ids=true, to_apply=%region_38.39 | all-reduce | flops 5892 | bytes 47136 | tf_op jit(solution)/shard_map/psum | solution.py:279
  571.1 1.8 fusion.196
  572.9 97.4 %all-reduce.41.cloned.1.call-done = (f32[256,256]{0,1:T(8,128)}, f32[256,256]{0,1:T(8,128)}, f32[256,512]{0,1:T(8,128)}, f32[256,512]{0,1:T(8,128)}, f32[512,256...) async-done(((f32[256,256]{0,1:T(8,128)}, f32[256,256]{0,1:T(8,128)}, f32[256,512]{0,1:T(8,128)}, f32[256,512]{0,1:T(8,128)}, ...) | async-done | bytes 4259856 | tf_op jit(solution)/shard_map/psum | solution.py:279
  670.3 1.9 copy.339
  672.2 1.8 copy.340
  674.0 2.1 copy.341
  (577 shorter events, 96.2 us)
Async XLA Ops:
  7.2 164.8 %copy-start = (bf16[704,256]{1,0:T(8,128)(2,1)S(1)}, bf16[704,256]{1,0:T(8,128)(2,1)}, u32[]{:S(2)}) copy-start(bf16[704,256]{1,0:T(8,128)(2,1)} %param.44) | copy-start | bytes 1081348
  7.2 86.8 %reduce-scatter.9.cloned.1.call-start = ((), (), s32[]{:S(2)}) async-start(), calls=%async_computation.8 | async-start | bytes 3952640 | tf_op jit(solution)/shard_map/reduce_scatter | solution.py:157
  34.7 7.5 %copy-start.130 = (f32[2]{0:T(128)S(1)}, f32[2]{0:T(128)}, u32[]{:S(2)}) copy-start(f32[2]{0:T(128)} %param.37) | copy-start | bytes 28
  34.8 7.6 %copy-start.113 = (f32[4,256]{1,0:T(4,128)S(1)}, f32[4,256]{1,0:T(4,128)}, u32[]{:S(2)}) copy-start(f32[4,256]{1,0:T(4,128)} %param.34) | copy-start | bytes 12292
  34.8 7.6 %copy-start.114 = (f32[4,256]{1,0:T(4,128)S(1)}, f32[4,256]{1,0:T(4,128)}, u32[]{:S(2)}) copy-start(f32[4,256]{1,0:T(4,128)} %param.35) | copy-start | bytes 12292
  34.8 7.6 %copy-start.104 = (f32[4,512]{1,0:T(4,128)S(1)}, f32[4,512]{1,0:T(4,128)}, u32[]{:S(2)}) copy-start(f32[4,512]{1,0:T(4,128)} %param.36) | copy-start | bytes 24580
  34.8 59.2 %copy-start.122 = (f32[2]{0:T(128)S(1)}, f32[2]{0:T(128)}, u32[]{:S(2)}) copy-start(f32[2]{0:T(128)} %param.38) | copy-start | bytes 28
  34.8 150.9 %reduce-scatter.11.cloned.1.call-start = ((), (), s32[]{:S(2)}) async-start(), calls=%async_computation.9 | async-start | bytes 655360 | tf_op jit(solution)/shard_map/reduce_scatter | solution.py:163
  35.4 112.3 %copy-start.69 = (f32[1,2,2,128]{3,1,2,0:T(2,128)}, f32[1,2,2,128]{3,1,2,0:T(2,128)S(1)}, u32[]{:S(2)}) copy-start(f32[1,2,2,128]{3,1,2,0:T(2,128)S(1)} %copy.434) | copy-start | bytes 6148
  42.3 56.9 %copy-start.124 = (f32[2]{0:T(128)}, f32[2]{0:T(128)S(1)}, u32[]{:S(2)}) copy-start(f32[2]{0:T(128)S(1)} %exponential_negate_fusion) | copy-start | bytes 28
  42.4 56.8 %copy-start.78 = (f32[1,256]{1,0:T(1,128)}, f32[1,256]{1,0:T(1,128)S(1)}, u32[]{:S(2)}) copy-start(f32[1,256]{1,0:T(1,128)S(1)} %get-tuple-element.2088) | copy-start | bytes 3076
  42.4 56.8 %copy-start.80 = (f32[1,256]{1,0:T(1,128)}, f32[1,256]{1,0:T(1,128)S(1)}, u32[]{:S(2)}) copy-start(f32[1,256]{1,0:T(1,128)S(1)} %get-tuple-element.2089) | copy-start | bytes 3076
  42.4 56.8 %copy-start.82 = (f32[1,256]{1,0:T(1,128)}, f32[1,256]{1,0:T(1,128)S(1)}, u32[]{:S(2)}) copy-start(f32[1,256]{1,0:T(1,128)S(1)} %get-tuple-element.2090) | copy-start | bytes 3076
  42.4 56.8 %copy-start.84 = (f32[1,256]{1,0:T(1,128)}, f32[1,256]{1,0:T(1,128)S(1)}, u32[]{:S(2)}) copy-start(f32[1,256]{1,0:T(1,128)S(1)} %get-tuple-element.2091) | copy-start | bytes 3076
  42.4 56.8 %copy-start.76 = (f32[1,256]{1,0:T(1,128)}, f32[1,256]{1,0:T(1,128)S(1)}, u32[]{:S(2)}) copy-start(f32[1,256]{1,0:T(1,128)S(1)} %get-tuple-element.2092) | copy-start | bytes 3076
  42.4 56.8 %copy-start.86 = (f32[1,256]{1,0:T(1,128)}, f32[1,256]{1,0:T(1,128)S(1)}, u32[]{:S(2)}) copy-start(f32[1,256]{1,0:T(1,128)S(1)} %get-tuple-element.2093) | copy-start | bytes 3076
  42.4 56.8 %copy-start.88 = (f32[1,256]{1,0:T(1,128)}, f32[1,256]{1,0:T(1,128)S(1)}, u32[]{:S(2)}) copy-start(f32[1,256]{1,0:T(1,128)S(1)} %get-tuple-element.2094) | copy-start | bytes 3076
  42.5 56.8 %copy-start.90 = (f32[1,256]{1,0:T(1,128)}, f32[1,256]{1,0:T(1,128)S(1)}, u32[]{:S(2)}) copy-start(f32[1,256]{1,0:T(1,128)S(1)} %get-tuple-element.2095) | copy-start | bytes 3076
  42.5 56.8 %copy-start.65 = (f32[1,512]{1,0:T(1,128)}, f32[1,512]{1,0:T(1,128)S(1)}, u32[]{:S(2)}) copy-start(f32[1,512]{1,0:T(1,128)S(1)} %get-tuple-element.2086) | copy-start | bytes 6148
  42.5 56.8 %copy-start.67 = (f32[1,512]{1,0:T(1,128)}, f32[1,512]{1,0:T(1,128)S(1)}, u32[]{:S(2)}) copy-start(f32[1,512]{1,0:T(1,128)S(1)} %get-tuple-element.2087) | copy-start | bytes 6148
  146.9 17.3 %copy-start.22 = (f32[2,2,64,256]{3,2,1,0:T(8,128)}, f32[2,2,64,256]{3,2,1,0:T(8,128)S(1)}, u32[]{:S(2)}) copy-start(f32[2,2,64,256]{3,2,1,0:T(8,128)S(1)} %get-tuple-element.2756) | copy-start | bytes 786436
  147.0 17.2 %copy-start.45 = (bf16[512,256]{1,0:T(8,128)(2,1)S(1)}, bf16[512,256]{1,0:T(8,128)(2,1)}, u32[]{:S(2)}) copy-start(bf16[512,256]{1,0:T(8,128)(2,1)} %param.40) | copy-start | bytes 786436
  147.7 17.7 %copy-start.97 = (f32[128,2]{0,1:T(2,128)}, f32[128,2]{0,1:T(2,128)S(1)}, u32[]{:S(2)}) copy-start(f32[128,2]{0,1:T(2,128)S(1)} %rsqrt.55) | copy-start | bytes 3076
  147.7 17.7 %copy-start.56 = (bf16[128,256]{1,0:T(8,128)(2,1)S(1)}, bf16[128,256]{1,0:T(8,128)(2,1)}, u32[]{:S(2)}) copy-start(bf16[128,256]{1,0:T(8,128)(2,1)} %param.45) | copy-start | bytes 196612
  165.4 58.1 %reduce-scatter.17.cloned.1.call-start = ((), (), s32[]{:S(2)}) async-start(), calls=%async_computation.12 | async-start | bytes 1966080 | tf_op jit(solution)/shard_map/reduce_scatter | solution.py:157
  173.5 12.2 %copy-start.20 = (bf16[128,256]{1,0:T(8,128)(2,1)S(1)}, bf16[128,256]{1,0:T(8,128)(2,1)}, u32[]{:S(2)}) copy-start(bf16[128,256]{1,0:T(8,128)(2,1)} %param.26) | copy-start | bytes 196612
  173.5 25.0 %copy-start.71 = (f32[256]{0:T(256)S(1)}, f32[256]{0:T(256)}, u32[]{:S(2)}) copy-start(f32[256]{0:T(256)} %param.41) | copy-start | bytes 3076
  173.5 107.3 %reduce-scatter.13.cloned.1.call-start = ((), (), s32[]{:S(2)}) async-start(), calls=%async_computation.10 | async-start | bytes 3604480 | tf_op jit(solution)/shard_map/reduce_scatter | solution.py:157
  186.7 168.8 %copy-start.6 = (f32[128,256]{1,0:T(8,128)}, f32[128,256]{1,0:T(8,128)S(1)}, u32[]{:S(2)}) copy-start(f32[128,256]{1,0:T(8,128)S(1)} %get-tuple-element.2002) | copy-start | bytes 393220
  198.5 157.0 %copy-start.105 = (f32[128]{0:T(128)}, f32[128]{0:T(128)S(1)}, u32[]{:S(2)}) copy-start(f32[128]{0:T(128)S(1)} %add_rsqrt_fusion.2) | copy-start | bytes 1540
  207.3 73.5 %copy-start.110 = (f32[128]{0:T(128)S(1)}, f32[128]{0:T(128)}, u32[]{:S(2)}) copy-start(f32[128]{0:T(128)} %subtract_convert_fusion.1) | copy-start | bytes 1540
  207.3 111.3 %all-gather.3.cloned.1.call-start = ((), (), s32[]{:S(2)}) async-start(), calls=%async_computation.13 | async-start | bytes 1802240 | tf_op jit(solution)/shard_map/all_gather | solution.py:146
  283.9 71.6 %copy-start.57 = (bf16[128,256]{1,0:T(8,128)(2,1)S(1)}, bf16[128,256]{1,0:T(8,128)(2,1)}, u32[]{:S(2)}) copy-start(bf16[128,256]{1,0:T(8,128)(2,1)} %param.45) | copy-start | bytes 196612
  284.0 58.3 %reduce-scatter.19.cloned.1.call-start = ((), (), s32[]{:S(2)}) async-start(), calls=%async_computation.14 | async-start | bytes 655360 | tf_op jit(solution)/shard_map/reduce_scatter | solution.py:163
  321.3 42.0 %copy-start.46 = (bf16[512,256]{1,0:T(8,128)(2,1)S(1)}, bf16[512,256]{1,0:T(8,128)(2,1)}, u32[]{:S(2)}) copy-start(bf16[512,256]{1,0:T(8,128)(2,1)} %param.40) | copy-start | bytes 786436
  321.4 68.0 %reduce-scatter.21.cloned.1.call-start = ((), (), s32[]{:S(2)}) async-start(), calls=%async_computation.15 | async-start | bytes 1310720 | tf_op jit(solution)/shard_map/reduce_scatter | solution.py:157
  355.5 9.2 %copy-start.126 = (f32[128]{0:T(128)}, f32[128]{0:T(128)S(1)}, u32[]{:S(2)}) copy-start(f32[128]{0:T(128)S(1)} %fusion.213) | copy-start | bytes 1540
  356.5 9.8 %copy-start.35 = (f32[128,256]{0,1:T(8,128)S(1)}, f32[128,256]{0,1:T(8,128)}, u32[]{:S(2)}) copy-start(f32[128,256]{0,1:T(8,128)} %copy-done.34) | copy-start | bytes 393220
  356.5 10.5 %copy-start.49 = (f32[128,512]{0,1:T(8,128)S(1)}, f32[128,512]{0,1:T(8,128)}, u32[]{:S(2)}) copy-start(f32[128,512]{0,1:T(8,128)} %get-tuple-element.2067) | copy-start | bytes 786436
  364.7 26.6 %copy-start.102 = (f32[256]{0:T(256)S(1)}, f32[256]{0:T(256)}, u32[]{:S(2)}) copy-start(f32[256]{0:T(256)} %param.39) | copy-start | bytes 3076
  364.8 141.3 %all-gather.5.cloned.1.call-start = ((), (), s32[]{:S(2)}) async-start(), calls=%async_computation.16 | async-start | bytes 1976320 | tf_op jit(solution)/shard_map/all_gather | solution.py:146
  390.5 8.5 %copy-start.5 = (f32[2,2,64,64]{3,2,1,0:T(8,128)S(1)}, f32[2,2,64,64]{3,2,1,0:T(8,128)}, u32[]{:S(2)}) copy-start(f32[2,2,64,64]{3,2,1,0:T(8,128)} %copy-done.4) | copy-start | bytes 196612
  416.8 7.6 %copy-start.62 = (f32[2,64,2]{2,1,0:T(8,128)S(1)}, f32[2,64,2]{2,1,0:T(8,128)}, u32[]{:S(2)}) copy-start(f32[2,64,2]{2,1,0:T(8,128)} %get-tuple-element.2771) | copy-start | bytes 3076 | tf_op jit(solution)/shard_map/transpose(jvp())/while
  442.9 5.5 copy-start.73
  442.9 7.6 %copy-start.62 = (f32[2,64,2]{2,1,0:T(8,128)S(1)}, f32[2,64,2]{2,1,0:T(8,128)}, u32[]{:S(2)}) copy-start(f32[2,64,2]{2,1,0:T(8,128)} %get-tuple-element.2771) | copy-start | bytes 3076 | tf_op jit(solution)/shard_map/transpose(jvp())/while
  451.2 6.7 copy-start.61
  451.2 6.8 copy-start.94
  451.2 7.7 %copy-start.44 = (f32[2,64,2,256]{3,1,2,0:T(8,128)S(1)}, f32[2,64,2,256]{3,1,2,0:T(8,128)}, u32[]{:S(2)}) copy-start(f32[2,64,2,256]{3,1,2,0:T(8,128)} %get-tuple-element.1072) | copy-start | bytes 786436
  465.5 40.6 %copy-start.3 = (bf16[256,1540]{1,0:T(8,128)(2,1)S(1)}, bf16[256,1540]{1,0:T(8,128)(2,1)}, u32[]{:S(2)}) copy-start(bf16[256,1540]{1,0:T(8,128)(2,1)} %copy-done.2) | copy-start | bytes 2365444
  469.6 39.5 %copy-start.54 = (bf16[128,704]{1,0:T(8,128)(2,1)S(1)}, bf16[128,704]{1,0:T(8,128)(2,1)}, u32[]{:S(2)}) copy-start(bf16[128,704]{1,0:T(8,128)(2,1)} %get-tuple-element.2072) | copy-start | bytes 540676
  469.6 67.2 %reduce-scatter.23.cloned.1.call-start = ((), (), s32[]{:S(2)}) async-start(), calls=%async_computation.17 | async-start | bytes 655360 | tf_op jit(solution)/shard_map/reduce_scatter | solution.py:163
  509.0 19.2 %copy-start.10 = (bf16[512,256]{1,0:T(8,128)(2,1)S(1)}, bf16[512,256]{1,0:T(8,128)(2,1)}, u32[]{:S(2)}) copy-start(bf16[512,256]{1,0:T(8,128)(2,1)} %copy-done.9) | copy-start | bytes 786436
  509.0 62.0 %reduce-scatter.15.cloned.1.call-start = ((), (), s32[]{:S(2)}) async-start(), calls=%async_computation.11 | async-start | bytes 655360 | tf_op jit(solution)/shard_map/reduce_scatter | solution.py:163
  529.4 140.9 %all-reduce.41.cloned.1.call-start = ((), (), s32[]{:S(2)}) async-start(), calls=%async_computation.18 | async-start | bytes 8781824 | tf_op jit(solution)/shard_map/psum | solution.py:279
  536.1 19.3 %copy-start.112 = (f32[256]{0:T(256)S(1)}, f32[256]{0:T(256)}, u32[]{:S(2)}) copy-start(f32[256]{0:T(256)} %get-tuple-element.1812) | copy-start | bytes 3076
  536.1 34.9 %copy-start.133 = (f32[128]{0:T(128)S(1)}, f32[128]{0:T(128)}, u32[]{:S(2)}) copy-start(f32[128]{0:T(128)} %copy-done.132) | copy-start | bytes 1540
  536.1 35.0 %copy-start.7 = (f32[128,256]{1,0:T(8,128)S(1)}, f32[128,256]{1,0:T(8,128)}, u32[]{:S(2)}) copy-start(f32[128,256]{1,0:T(8,128)} %copy-done.6) | copy-start | bytes 393220
  536.1 35.0 %copy-start.31 = (f32[128,256]{1,0:T(8,128)S(1)}, f32[128,256]{1,0:T(8,128)}, u32[]{:S(2)}) copy-start(f32[128,256]{1,0:T(8,128)} %reduce-scatter.19.cloned.1.call-done) | copy-start | bytes 393220
  536.1 35.0 %copy-start.58 = (bf16[128,256]{1,0:T(8,128)(2,1)S(1)}, bf16[128,256]{1,0:T(8,128)(2,1)}, u32[]{:S(2)}) copy-start(bf16[128,256]{1,0:T(8,128)(2,1)} %param.45) | copy-start | bytes 196612
  536.1 35.0 %copy-start.72 = (f32[256]{0:T(256)S(1)}, f32[256]{0:T(256)}, u32[]{:S(2)}) copy-start(f32[256]{0:T(256)} %param.41) | copy-start | bytes 3076
  536.1 35.0 %copy-start.106 = (f32[128]{0:T(128)S(1)}, f32[128]{0:T(128)}, u32[]{:S(2)}) copy-start(f32[128]{0:T(128)} %copy-done.105) | copy-start | bytes 1540
  536.1 35.0 %copy-start.127 = (f32[128]{0:T(128)S(1)}, f32[128]{0:T(128)}, u32[]{:S(2)}) copy-start(f32[128]{0:T(128)} %copy-done.126) | copy-start | bytes 1540
  670.3 5.8 copy-start.60
  670.3 6.8 copy-start.53
  (94 other events, 254.0 us)
Sparse Core Ops, SparseCore 0:
  34.9 59.0 reduce-scatter.8
  165.5 20.1 reduce-scatter.10
  188.0 35.4 reduce-scatter.16
  225.7 55.1 reduce-scatter.12
  284.1 34.5 all-gather.2
  321.5 20.6 reduce-scatter.18
  364.9 24.5 reduce-scatter.20
  469.7 36.3 all-gather.4
  509.1 19.8 reduce-scatter.22
  531.9 21.6 reduce-scatter.14
  557.9 112.3 all-reduce.40
where the time goes:
time: 689 us; the launch traced here: 687 us
  waiting for transfers between devices  346 us (50%)
  blocking collectives  126 us (18%)
  other arithmetic  92.5 us (13%)
  local copies, waits for them, and re-layouts  62.5 us (9%)
  matrix products  42.3 us (6%)
  between operations  15.8 us (2%)
    reduce_scatter x4, waiting for transfers between devices, head_sums(): lax.psum_scatter(product_terms(left, right, flipped), 'row', scatter_dime...  146 us
    psum x1, waiting for transfers between devices, shards(): lax.psum((gain_sums[0], in_grads[0], in_grads[1], in_grads[2], in_grads[3...  97.4 us
    all_gather x2, waiting for transfers between devices, head_gather(): return lax.all_gather(values, 'row', axis=0, tiled=True)  70.8 us
    psum x4, blocking collectives, feature_total(): return lax.psum(values, 'row')  54.3 us
    another operation x18, other arithmetic, advance(): jax.scipy.linalg.solve_triangular(lower_part, target, lower=True, unit_di...  39.8 us
    all_gather x2, blocking collectives, head_gather(): return lax.all_gather(values, 'row', axis=0, tiled=True)  32.7 us
    reduce_scatter x4, waiting for transfers between devices, token_sums(): lax.psum_scatter(product_terms(left, right, flipped), 'col', scatter_dime...  30.9 us
    all_gather x4, blocking collectives, token_gather(): return lax.all_gather(values, 'col', axis=0, tiled=True)  23.4 us
  transfers between devices with their start and end apart: 11, of which 9 were waited for; matrix products, arithmetic and copies ran while one was open for 4% of the time, Pallas kernels for 0%

commit v1 on v0

v1 whole, which is shorter than its diff:
```python
import jax
import jax.numpy as jnp
from jax import lax
from jax.experimental import pallas as pl
from jax.experimental.pallas import tpu as pltpu
from jax.sharding import PartitionSpec as P

epsilon = 1e-06
highest = lax.Precision.HIGHEST


def fp_dot(left, right, left_dim, right_dim):
    return lax.dot_general(
        left,
        right,
        (((left_dim,), (right_dim,)), ((), ())),
        precision=highest,
        preferred_element_type=jnp.float32,
    )


def plain_softplus(values):
    return jnp.maximum(values, 0.0) + jnp.log1p(jnp.exp(-jnp.abs(values)))


@jax.custom_vjp
def smooth_ramp(values):
    return plain_softplus(values)


smooth_ramp.defvjp(
    lambda values: (plain_softplus(values), values),
    lambda values, upstream: (upstream * lax.logistic(values),),
)


@jax.custom_vjp
def apply_inverse(inverse, lower_part, target):
    return fp_dot(inverse, target, 1, 0)


def apply_inverse_forward(inverse, lower_part, target):
    writes = fp_dot(inverse, target, 1, 0)
    return writes, (inverse, writes)


def apply_inverse_backward(saved, upstream):
    inverse, writes = saved
    grad_target = fp_dot(inverse, upstream, 0, 0)
    return (jnp.zeros_like(inverse), -fp_dot(grad_target, writes, 1, 1), grad_target)


apply_inverse.defvjp(apply_inverse_forward, apply_inverse_backward)


def unit_lower_inverse(lower_part, row_index, column_index):
    length = lower_part.shape[0]
    inverse = jnp.where(row_index == column_index, 1.0, 0.0)
    level = 0
    while (1 << level) < length:
        row_block = row_index >> level
        column_block = column_index >> level
        joined = (row_block == column_block + 1) & ((column_block & 1) == 0)
        corner = jnp.where(joined, lower_part, 0.0)
        if level == 0:
            inverse = inverse - corner
        else:
            inverse = inverse - fp_dot(fp_dot(inverse, corner, 1, 0), inverse, 1, 0)
        level += 1
    return inverse


def slot_masks(bounds_ref, length, tap_count):
    row_index = lax.broadcasted_iota(jnp.int32, (length, length), 0)
    column_index = lax.broadcasted_iota(jnp.int32, (length, length), 1)
    token = lax.broadcasted_iota(jnp.int32, (length, 1), 0)
    row_segment = jnp.zeros((length, length), jnp.int32)
    column_segment = jnp.zeros((length, length), jnp.int32)
    inside = jnp.zeros((length, 1), jnp.float32)
    for i in range(bounds_ref.shape[1]):
        begin = bounds_ref[0, i]
        end = begin + bounds_ref[1, i]
        row_segment += jnp.where(row_index >= begin, 1, 0) + jnp.where(row_index >= end, 1, 0)
        column_segment += jnp.where(column_index >= begin, 1, 0)
        column_segment += jnp.where(column_index >= end, 1, 0)
        inside += jnp.where((token >= begin) & (token < end), 1.0, 0.0)
    same = row_segment == column_segment
    shifts = [
        jnp.where(same & (column_index == row_index - offset), 1.0, 0.0)
        for offset in range(1, tap_count)
    ]
    return dict(
        row_index=row_index,
        column_index=column_index,
        shifts=shifts,
        strict=jnp.where(same & (row_index > column_index), 1.0, 0.0),
        within=jnp.where(same & (row_index >= column_index), 1.0, 0.0),
        upto=jnp.where(row_index >= column_index, 1.0, 0.0),
        later=jnp.where(row_index > column_index, 1.0, 0.0),
        inside=inside,
    )


def conv_head(signal, taps, shifts):
    total = taps[-1] * signal
    for offset, shift in enumerate(shifts, 1):
        total = total + taps[len(taps) - 1 - offset] * fp_dot(shift, signal, 1, 0)
    return total * lax.logistic(total)


def unit_rows(values):
    return values * lax.rsqrt(jnp.sum(values * values, axis=1, keepdims=True) + epsilon)


def mixer_head(masks, inverse, bias, linears, taps, rate, norm_gain):
    query_lin, key_lin, value_lin, gate_lin, decay_lin, rate_lin = linears
    differentiated = inverse is not None
    queries = unit_rows(conv_head(query_lin, taps[0], masks["shifts"]))
    queries = queries * queries.shape[1] ** (-0.5)
    keys = unit_rows(conv_head(key_lin, taps[1], masks["shifts"]))
    values = conv_head(value_lin, taps[2], masks["shifts"])
    write_rate = lax.logistic(rate_lin)
    ramp = smooth_ramp if differentiated else plain_softplus
    log_decay = -rate * ramp(decay_lin + bias)
    ratio = jnp.exp(fp_dot(masks["upto"], log_decay * masks["later"], 1, 0))
    lower_part = write_rate * ratio * fp_dot(keys, keys, 1, 1) * masks["strict"]
    target = write_rate * values
    if differentiated:
        writes = apply_inverse(inverse, lower_part, target)
    else:
        inverse = unit_lower_inverse(lower_part, masks["row_index"], masks["column_index"])
        writes = fp_dot(inverse, target, 1, 0)
    heads = fp_dot(ratio * fp_dot(queries, keys, 1, 1) * masks["within"], writes, 1, 0)
    mean_square = jnp.sum(heads * heads, axis=1, keepdims=True) * (1.0 / heads.shape[1])
    normed = heads * lax.rsqrt(mean_square + epsilon) * norm_gain
    gated = normed * (gate_lin * lax.logistic(gate_lin)) * masks["inside"]
    return (gated, inverse)


def head_operands(h, heads, lin_ref, conv_refs, log_ref, bias_ref, gain_ref):
    length = lin_ref.shape[0]
    key_size = conv_refs[0].shape[1] // heads
    value_size = conv_refs[2].shape[1] // heads
    widths = (key_size, key_size, value_size, value_size)
    spans = []
    base = 0
    for width in widths:
        spans.append(slice(base + h * width, base + (h + 1) * width))
        base += heads * width
    tail = lin_ref[:, base : base + 2 * heads]
    lane = lax.broadcasted_iota(jnp.int32, tail.shape, 1)
    columns = [
        jnp.sum(jnp.where(lane == place, tail, 0.0), axis=1, keepdims=True)
        for place in (h, heads + h)
    ]
    linears = tuple(lin_ref[:, span] for span in spans) + tuple(columns)
    tap_spans = [slice(h * width, (h + 1) * width) for width in widths[:3]]
    taps = tuple(
        tuple(ref[i : i + 1, span] for i in range(ref.shape[0]))
        for ref, span in zip(conv_refs, tap_spans)
    )
    rate = jnp.exp(jnp.full((length, 1), log_ref[h], jnp.float32))
    bias = jnp.full((length, 1), bias_ref[h], jnp.float32)
    return linears, taps, rate, bias, gain_ref[...], spans, tap_spans, base


def spread_columns(columns):
    shape = (columns[0].shape[0], len(columns))
    lane = lax.broadcasted_iota(jnp.int32, shape, 1)
    total = jnp.zeros(shape, jnp.float32)
    for place, column in enumerate(columns):
        total = total + jnp.where(lane == place, column, 0.0)
    return total


def mixer_forward_kernel(
    bounds_ref, log_ref, bias_ref, lin_ref, qc_ref, kc_ref, vc_ref, gain_ref, out_ref, inverse_ref
):
    heads = log_ref.shape[0]
    conv_refs = (qc_ref, kc_ref, vc_ref)
    masks = slot_masks(bounds_ref, lin_ref.shape[0], qc_ref.shape[0])
    for h in range(heads):
        linears, taps, rate, bias, gain, _, tap_spans, _ = head_operands(
            h, heads, lin_ref, conv_refs, log_ref, bias_ref, gain_ref
        )
        gated, inverse = mixer_head(masks, None, bias, linears, taps, rate, gain)
        out_ref[:, tap_spans[2]] = gated.astype(out_ref.dtype)
        inverse_ref[h] = inverse


def mixer_backward_kernel(
    bounds_ref,
    log_ref,
    bias_ref,
    lin_ref,
    qc_ref,
    kc_ref,
    vc_ref,
    gain_ref,
    inverse_ref,
    upstream_ref,
    wire_ref,
    dq_ref,
    dk_ref,
    dv_ref,
    gain_grad_ref,
    column_ref,
):
    heads = log_ref.shape[0]
    conv_refs = (qc_ref, kc_ref, vc_ref)
    masks = slot_masks(bounds_ref, lin_ref.shape[0], qc_ref.shape[0])
    decay_columns, rate_columns, log_columns = [], [], []
    gain_total = jnp.zeros(gain_ref.shape, jnp.float32)
    for h in range(heads):
        linears, taps, rate, bias, gain, spans, tap_spans, base = head_operands(
            h, heads, lin_ref, conv_refs, log_ref, bias_ref, gain_ref
        )
        inverse = inverse_ref[h]

        def piece(linear_set, tap_set, rate_set, gain_set):
            return mixer_head(masks, inverse, bias, linear_set, tap_set, rate_set, gain_set)[0]

        _, back = jax.vjp(piece, linears, taps, rate, gain)
        grad_linears, grad_taps, grad_rate, grad_gain = back(upstream_ref[:, tap_spans[2]])
        for span, grad in zip(spans, grad_linears):
            wire_ref[:, span] = grad.astype(wire_ref.dtype)
        for ref, span, grads in zip((dq_ref, dk_ref, dv_ref), tap_spans, grad_taps):
            for i, grad in enumerate(grads):
                ref[i : i + 1, span] = grad
        gain_total = gain_total + grad_gain
        decay_columns.append(grad_linears[4])
        rate_columns.append(grad_linears[5])
        log_columns.append(grad_rate * rate)
    wire_ref[:, base : base + 2 * heads] = spread_columns(decay_columns + rate_columns).astype(
        wire_ref.dtype
    )
    column_ref[...] = spread_columns(log_columns + decay_columns)
    gain_grad_ref[...] = gain_total


def mixer_specs(count):
    return [pl.BlockSpec(memory_space=pltpu.SMEM)] * 3 + [
        pl.BlockSpec(memory_space=pltpu.VMEM)
    ] * count


def mixer_forward(bounds, projected, params):
    conv_query, conv_key, conv_value, log_rate, rate_bias, norm_gain = params
    length = projected.shape[0]
    heads = log_rate.shape[0]
    return pl.pallas_call(
        mixer_forward_kernel,
        out_shape=(
            jax.ShapeDtypeStruct((length, conv_value.shape[1]), jnp.bfloat16),
            jax.ShapeDtypeStruct((heads, length, length), jnp.float32),
        ),
        in_specs=mixer_specs(5),
        out_specs=tuple(mixer_specs(2)[3:]),
        name="mixer_forward",
    )(bounds, log_rate, rate_bias, projected, conv_query, conv_key, conv_value, norm_gain[None, :])


def mixer_backward(bounds, projected, params, inverse, upstream):
    conv_query, conv_key, conv_value, log_rate, rate_bias, norm_gain = params
    length = projected.shape[0]
    heads = log_rate.shape[0]
    wire, dq, dk, dv, dgain, columns = pl.pallas_call(
        mixer_backward_kernel,
        out_shape=(
            jax.ShapeDtypeStruct(projected.shape, jnp.bfloat16),
            jax.ShapeDtypeStruct(conv_query.shape, jnp.float32),
            jax.ShapeDtypeStruct(conv_key.shape, jnp.float32),
            jax.ShapeDtypeStruct(conv_value.shape, jnp.float32),
            jax.ShapeDtypeStruct((1, norm_gain.shape[0]), jnp.float32),
            jax.ShapeDtypeStruct((length, 2 * heads), jnp.float32),
        ),
        in_specs=mixer_specs(7),
        out_specs=tuple(mixer_specs(6)[3:]),
        name="mixer_backward",
    )(
        bounds,
        log_rate,
        rate_bias,
        projected,
        conv_query,
        conv_key,
        conv_value,
        norm_gain[None, :],
        inverse,
        upstream,
    )
    sums = jnp.sum(columns, axis=0)
    return wire, (dq, dk, dv, sums[:heads], sums[heads:], dgain[0])


def small_sum(values, axes):
    return jnp.sum(lax.all_gather(values, axes), axis=0)


def feature_total(values):
    return small_sum(values, "row")


def norm_scale(values):
    feature_count = values.shape[1] * lax.axis_size("row")
    return lax.rsqrt(feature_total(jnp.sum(values * values, axis=1)) / feature_count + epsilon)


def norm_backward(values, row_scale, gain_vector, upstream):
    feature_count = values.shape[1] * lax.axis_size("row")
    weighted = upstream * gain_vector
    inner_mean = feature_total(jnp.sum(weighted * values, axis=1)) / feature_count
    grad_values = (
        row_scale[:, None] * weighted
        - values * (row_scale * row_scale * row_scale * inner_mean)[:, None]
    )
    return (grad_values, jnp.sum(upstream * values * row_scale[:, None], axis=0))


def token_gather(values):
    return lax.all_gather(values, "col", axis=0, tiled=True)


def head_gather(values):
    return lax.all_gather(values, "row", axis=0, tiled=True)


def product_terms(left, right, flipped):
    inner_dim = 1 if flipped else 0
    return lax.dot_general(
        left, right, (((1,), (inner_dim,)), ((), ())), preferred_element_type=jnp.float32
    )


def head_sums(left, right, flipped):
    terms = product_terms(left, right, flipped)
    return lax.psum_scatter(terms, "row", scatter_dimension=0, tiled=True)


def token_sums(left, right, flipped):
    terms = product_terms(left, right, flipped)
    return lax.psum_scatter(terms, "col", scatter_dimension=0, tiled=True)


def group_sum(values):
    sent = values.astype(jnp.bfloat16)
    if lax.axis_size("dp") == 2:
        other = lax.ppermute(sent, "dp", [(0, 1), (1, 0)])
        return sent.astype(jnp.float32) + other.astype(jnp.float32)
    return lax.psum(sent, "dp").astype(jnp.float32)


def packed_psum(arrays, axes):
    flat = jnp.concatenate([array.reshape(-1) for array in arrays])
    total = small_sum(flat, axes)
    pieces = []
    start = 0
    for array in arrays:
        pieces.append(total[start : start + array.size].reshape(array.shape))
        start += array.size
    return pieces


def weight_grad(left, right):
    return lax.dot_general(
        left, right, (((0,), (0,)), ((), ())), preferred_element_type=jnp.float32
    )


def split_points(matrices):
    edges = []
    running_total = 0
    for matrix in matrices[:-1]:
        running_total = running_total + matrix.shape[1]
        edges.append(running_total)
    return edges


def shards(
    block_input,
    attn_gain,
    query_weight,
    key_weight,
    value_weight,
    gate_weight,
    decay_weight,
    beta_weight,
    query_conv,
    key_conv,
    value_conv,
    decay_log,
    decay_bias,
    head_gain,
    out_weight,
    ffn_gain,
    ffn_gate,
    ffn_up,
    ffn_down,
    out_grad,
    seq_starts,
    seq_lengths,
):
    slot_rows = block_input.shape[0]
    slot_index = lax.axis_index("dp") * lax.axis_size("col") + lax.axis_index("row")
    starts = lax.dynamic_index_in_dim(seq_starts, slot_index, 0, keepdims=False)
    lengths = lax.dynamic_index_in_dim(seq_lengths, slot_index, 0, keepdims=False)
    bounds = jnp.stack([starts, lengths])
    position = jnp.arange(slot_rows, dtype=jnp.int32)[:, None]
    inside = jnp.sum(
        ((position >= starts) & (position < starts + lengths)).astype(jnp.float32), axis=1
    )
    inputs = block_input.astype(jnp.float32)
    first_scale = norm_scale(inputs)
    first_normalized = (inputs * first_scale[:, None] * attn_gain).astype(jnp.bfloat16)
    gathered_first = token_gather(first_normalized)
    in_list = (query_weight, key_weight, value_weight, gate_weight, decay_weight, beta_weight)
    in_edges = split_points(in_list)
    in_weights = jnp.concatenate(in_list, axis=1)
    projected = head_sums(gathered_first, in_weights, False)
    mixer_params = (query_conv, key_conv, value_conv, decay_log, decay_bias, head_gain)
    mixer_output, inverse = mixer_forward(bounds, projected, mixer_params)
    mixed_rows = head_gather(mixer_output)
    resid = inputs + token_sums(mixed_rows, out_weight, False)
    second_scale = norm_scale(resid)
    second_normalized = (resid * second_scale[:, None] * ffn_gain).astype(jnp.bfloat16)
    gathered_second = token_gather(second_normalized)
    ffn_weights = jnp.concatenate([ffn_gate, ffn_up], axis=1)
    hidden_width = ffn_gate.shape[1]
    ffn_inner = head_sums(gathered_second, ffn_weights, False)
    gate_part = ffn_inner[:, :hidden_width]
    up_part = ffn_inner[:, hidden_width:]
    hidden_activation = (jax.nn.silu(gate_part) * up_part * inside[:, None]).astype(jnp.bfloat16)
    hidden_rows = head_gather(hidden_activation)
    output = (resid + token_sums(hidden_rows, ffn_down, False)).astype(jnp.bfloat16)
    grad_rows = token_gather(out_grad)
    down_grad = weight_grad(hidden_rows, grad_rows)
    grad_hidden = head_sums(grad_rows, ffn_down, True) * inside[:, None]
    sigmoid_gate = jax.nn.sigmoid(gate_part)
    gate_gradient = grad_hidden * up_part * sigmoid_gate * (1.0 + gate_part * (1.0 - sigmoid_gate))
    up_gradient = grad_hidden * gate_part * sigmoid_gate
    grad_ffn = jnp.concatenate([gate_gradient, up_gradient], axis=1).astype(jnp.bfloat16)
    grad_ffn_rows = head_gather(grad_ffn)
    ffn_weight_grad = weight_grad(gathered_second, grad_ffn_rows)
    gate_grad = ffn_weight_grad[:, :hidden_width]
    up_grad = ffn_weight_grad[:, hidden_width:]
    grad_second = token_sums(grad_ffn_rows, ffn_weights, True)
    resid_part, feedforward_gain_share = norm_backward(resid, second_scale, ffn_gain, grad_second)
    grad_resid = out_grad.astype(jnp.float32) + resid_part
    residual_signal_path = grad_resid.astype(jnp.bfloat16)
    resid_rows = token_gather(residual_signal_path)
    out_weight_grad = weight_grad(mixed_rows, resid_rows)
    grad_mixed = head_sums(resid_rows, out_weight, True)
    linear_signal_path, parameter_gradients = mixer_backward(
        bounds, projected, mixer_params, inverse, grad_mixed
    )
    lin_rows = head_gather(linear_signal_path)
    in_weight_grad = weight_grad(gathered_first, lin_rows)
    in_grads = jnp.split(in_weight_grad, in_edges, axis=1)
    grad_first = token_sums(lin_rows, in_weights, True)
    input_part, attention_gain_share = norm_backward(inputs, first_scale, attn_gain, grad_first)
    input_grad = grad_resid + input_part
    param_sums = packed_psum(parameter_gradients, ("dp", "row"))
    gain_sums = packed_psum((attention_gain_share, feedforward_gain_share), ("dp", "col"))
    head_gain_grad = small_sum(param_sums[5], "col")
    return (
        output,
        input_grad,
        gain_sums[0],
        *[group_sum(grad) for grad in in_grads],
        *param_sums[:5],
        head_gain_grad,
        group_sum(out_weight_grad),
        gain_sums[1],
        group_sum(gate_grad),
        group_sum(up_grad),
        group_sum(down_grad),
    )


def solution(mesh):
    in_specs = (
        P(("dp", "col"), "row"),
        P("row"),
        P("row", "col"),
        P("row", "col"),
        P("row", "col"),
        P("row", "col"),
        P("row", "col"),
        P("row", "col"),
        P(None, "col"),
        P(None, "col"),
        P(None, "col"),
        P("col"),
        P("col"),
        P(),
        P("col", "row"),
        P("row"),
        P("row", "col"),
        P("row", "col"),
        P("col", "row"),
        P(("dp", "col"), "row"),
        P(),
        P(),
    )
    out_specs = (
        P(("dp", "col"), "row"),
        P(("dp", "col"), "row"),
        P("row"),
        P("row", "col"),
        P("row", "col"),
        P("row", "col"),
        P("row", "col"),
        P("row", "col"),
        P("row", "col"),
        P(None, "col"),
        P(None, "col"),
        P(None, "col"),
        P("col"),
        P("col"),
        P(),
        P("col", "row"),
        P("row"),
        P("row", "col"),
        P("row", "col"),
        P("col", "row"),
    )
    return jax.shard_map(shards, mesh=mesh, in_specs=in_specs, out_specs=out_specs, check_vma=False)
```

time: 689 us -> 531 us (0.77)
  other arithmetic: 92.5 us -> 20.2 us
  local copies, waits for them, and re-layouts: 62.5 us -> 21.5 us
  waiting for transfers between devices: 346 us -> 305 us
  matrix products: 42.3 us -> 19.9 us
  Pallas kernels: 0 us -> 20.3 us
  starting transfers between devices: 0.68 us -> 11.8 us
  blocking collectives: 126 us -> 116 us
    psum x1 -> x0, waiting for transfers between devices: 97.4 us -> none  [shards(): lax.psum((gain_sums[0], in_grads[0], in_grads[1], in_grads[2], in_grads[3...]
    psum x6 -> x0, blocking collectives: 70 us -> none  [the longest x4 54.3 us: feature_total(): return lax.psum(values, 'row')]
    all_gather x0 -> x6, blocking collectives: none -> 58.5 us  [small_sum(): return jnp.sum(lax.all_gather(values, axes), axis=0)]
    another operation x50 -> x2, other arithmetic: 45.1 us -> 3.38 us  [the longest x1 1.86 us: shards(): bounds = jnp.stack([starts, lengths])]
    ppermute x0 -> x10, waiting for transfers between devices: none -> 30.8 us  [group_sum(): other = lax.ppermute(sent, 'dp', [(0, 1), (1, 0)])]
    pallas_call x0 -> x2, Pallas kernels: none -> 20.3 us  [the longest x1 10.2 us: mixer_backward(): pl.pallas_call(mixer_backward_kernel, out_shape=(jax.ShapeDtypeStruct(pro...]
    dot_general x38 -> x0, matrix products: 19.5 us -> none  [the longest x6 4.04 us: advance(): jnp.einsum('hvk,thk->htv', memory, block_query, precision=highest)]
    unnamed x11 -> x12, waiting for transfers between devices: 0.18 us -> 17 us
  transfers between devices with their start and end apart: 11 -> 21, of which waited for: 9 -> 16; matrix products, arithmetic and copies ran while one was open for 4% -> 8% of each run, Pallas kernels for 0% -> 0%
where the time goes in v1:
time: 531 us
  waiting for transfers between devices  305 us (57%)
  blocking collectives  116 us (22%)
  local copies, waits for them, and re-layouts  21.5 us (4%)
  Pallas kernels  20.3 us (4%)
  other arithmetic  20.2 us (4%)
  matrix products  19.9 us (4%)
  between operations  16.2 us (3%)
  starting transfers between devices  11.8 us (2%)
    reduce_scatter x4, waiting for transfers between devices, head_sums(): return lax.psum_scatter(terms, 'row', scatter_dimension=0, tiled=True)  157 us
    all_gather x2, waiting for transfers between devices, head_gather(): return lax.all_gather(values, 'row', axis=0, tiled=True)  66.2 us
    all_gather x6, blocking collectives, small_sum(): return jnp.sum(lax.all_gather(values, axes), axis=0)  58.5 us
    all_gather x2, blocking collectives, head_gather(): return lax.all_gather(values, 'row', axis=0, tiled=True)  34.1 us
    reduce_scatter x4, waiting for transfers between devices, token_sums(): return lax.psum_scatter(terms, 'col', scatter_dimension=0, tiled=True)  33.6 us
    ppermute x10, waiting for transfers between devices, group_sum(): other = lax.ppermute(sent, 'dp', [(0, 1), (1, 0)])  30.8 us
    all_gather x4, blocking collectives, token_gather(): return lax.all_gather(values, 'col', axis=0, tiled=True)  23.1 us
    unnamed x12, waiting for transfers between devices  17 us
  transfers between devices with their start and end apart: 21, of which 16 were waited for; matrix products, arithmetic and copies ran while one was open for 8% of the time, Pallas kernels for 0%

profile of v1, /device:TPU:0, one launch (start us, length us, event | category | flops | bytes accessed | tf_op | source)
XLA Modules:
  0.0 530.5 jit_solution(18072117371122872817)
XLA Ops:
  7.3 1.0 fusion
  8.2 12.6 %all-gather.7 = f32[4,1,128]{2,1,0:T(1,128)S(1)} all-gather(f32[1,1,128]{2,1,0:T(1,128)S(1)} %bitcast.57), channel_id=2, replica_groups=mesh['dp'=2,'row'=4,'col'=4] {'row'}, dimensions={0}, use_global_device_ids=true | all-gather | bytes 2560 | tf_op jit(solution)/shard_map/all_gather | solution.py:297
  21.8 5.8 %all_gather.68 = bf16[512,256]{1,0:T(8,128)(2,1)S(1)} all-gather(bf16[128,256]{1,0:T(8,128)(2,1)S(1)} %fusion.2), channel_id=1, replica_groups=mesh['dp'=2,'row'=4,'col'=4] {'col'}, dimensions={0}, use_global_device_ids=true | all-gather | bytes 327680 | tf_op jit(solution)/shard_map/all_gather | solution.py:321
  29.3 1.3 concatenate.17
  30.6 2.4 fusion.18
  34.2 1.9 pad_add_fusion.bounds_ref
  36.1 59.7 %reduce-scatter.9.cloned.1.call-done.lin_ref = f32[128,1540]{1,0:T(8,128)} async-done(((f32[512,1540]{1,0:T(8,128)}), f32[128,1540]{1,0:T(8,128)}) %reduce-scatter.9.cloned.1.call-update) | async-done | bytes 788496 | tf_op jit(solution)/shard_map/reduce_scatter | solution.py:337
  95.8 10.1 %mixer_forward.1 = (bf16[128,512]{1,0:T(8,128)(2,1)}, f32[2,128,128]{2,1,0:T(8,128)}) custom-call(s32[2,1]{1,0:T(2,128)} %pad_add_fusion.bounds_ref, f32[2]{0:T(128)} %log_ref.3, f32[2]{0:T(128)} %bias_ref.3, f32[128,1540]{1,0:T(8,128)} %reduce-scatter.9.cloned.1.call-done.lin_ref, f32[4,256]{1,0:T(4,128)} %qc_ref.3, f32[4,256]{1,0:T(4,128)} %kc_ref.3, ...), custom_call_target="tpu_custom_call" | custom-call | tf_op jit(solution)/shard_map/mixer_forward/pallas_call | solution.py:251
  105.9 15.5 %all_gather.69 = bf16[512,512]{1,0:T(8,128)(2,1)S(1)} all-gather(bf16[128,512]{1,0:T(8,128)(2,1)} %get-tuple-element.28), channel_id=1, replica_groups=mesh['dp'=2,'row'=4,'col'=4] {'row'}, dimensions={0}, use_global_device_ids=true | all-gather | bytes 655360 | tf_op jit(solution)/shard_map/all_gather | solution.py:325
  122.2 1.1 fusion.19
  123.4 5.8 %all_gather.74 = bf16[512,256]{1,0:T(8,128)(2,1)S(1)} all-gather(bf16[128,256]{1,0:T(8,128)(2,1)S(1)} %copy-done.12), channel_id=1, replica_groups=mesh['dp'=2,'row'=4,'col'=4] {'col'}, dimensions={0}, use_global_device_ids=true | all-gather | bytes 327680 | tf_op jit(solution)/shard_map/all_gather | solution.py:321
  129.9 1.6 fusion.22
  131.6 1.0 constant_dynamic-update-slice_fusion
  132.6 12.9 %reduce-scatter.11.cloned.1.call-done = f32[128,256]{1,0:T(8,128)} async-done(((f32[512,256]{1,0:T(8,128)}), f32[128,256]{1,0:T(8,128)}) %reduce-scatter.11.cloned.1.call-update) | async-done | bytes 131088 | tf_op jit(solution)/shard_map/reduce_scatter | solution.py:342
  145.5 1.0 multiply_reduce_fusion.2
  146.5 10.9 %all-gather.8 = f32[4,1,128]{2,1,0:T(1,128)S(1)} all-gather(f32[1,1,128]{2,1,0:T(1,128)S(1)} %bitcast.54), channel_id=3, replica_groups=mesh['dp'=2,'row'=4,'col'=4] {'row'}, dimensions={0}, use_global_device_ids=true | all-gather | bytes 2560 | tf_op jit(solution)/shard_map/all_gather | solution.py:297
  157.5 5.8 %all_gather.72 = bf16[512,256]{1,0:T(8,128)(2,1)S(1)} all-gather(bf16[128,256]{1,0:T(8,128)(2,1)S(1)} %multiply_convert_fusion.3), channel_id=1, replica_groups=mesh['dp'=2,'row'=4,'col'=4] {'col'}, dimensions={0}, use_global_device_ids=true | all-gather | bytes 327680 | tf_op jit(solution)/shard_map/all_gather | solution.py:321
  163.3 2.2 fusion.20
  167.5 15.7 %reduce-scatter.17.cloned.1.call-done = f32[128,704]{1,0:T(8,128)} async-done(((f32[512,704]{1,0:T(8,128)}), f32[128,704]{1,0:T(8,128)}) %reduce-scatter.17.cloned.1.call-update) | async-done | bytes 360464 | tf_op jit(solution)/shard_map/reduce_scatter | solution.py:337
  183.3 57.4 %reduce-scatter.13.cloned.1.call-done = f32[128,1408]{1,0:T(8,128)} async-done(((f32[512,1408]{1,0:T(8,128)}), f32[128,1408]{1,0:T(8,128)}) %reduce-scatter.13.cloned.1.call-update) | async-done | bytes 720912 | tf_op jit(solution)/shard_map/reduce_scatter | solution.py:337
  240.6 1.5 multiply_convert_fusion.1
  243.1 34.6 %all-gather.16.cloned.1.call-done = bf16[512,1408]{1,0:T(8,128)(2,1)} async-done(((bf16[128,1408]{1,0:T(8,128)(2,1)}), bf16[512,1408]{1,0:T(8,128)(2,1)}) %all-gather.16.cloned.1.call-update) | async-done | bytes 1441808 | tf_op jit(solution)/shard_map/all_gather | solution.py:325
  277.7 2.7 fusion.23
  280.5 20.8 %reduce-scatter.19.cloned.1.call-done = f32[128,256]{1,0:T(8,128)} async-done(((f32[512,256]{1,0:T(8,128)}), f32[128,256]{1,0:T(8,128)}) %reduce-scatter.19.cloned.1.call-update) | async-done | bytes 131088 | tf_op jit(solution)/shard_map/reduce_scatter | solution.py:342
  301.3 1.0 multiply_reduce_fusion
  302.3 10.9 %all-gather.9 = f32[4,1,128]{2,1,0:T(1,128)S(1)} all-gather(f32[1,1,128]{2,1,0:T(1,128)S(1)} %bitcast.55), channel_id=4, replica_groups=mesh['dp'=2,'row'=4,'col'=4] {'row'}, dimensions={0}, use_global_device_ids=true | all-gather | bytes 2560 | tf_op jit(solution)/shard_map/all_gather | solution.py:297
  313.2 1.0 fusion.10
  314.3 5.8 %all_gather.78 = bf16[512,256]{1,0:T(8,128)(2,1)S(1)} all-gather(bf16[128,256]{1,0:T(8,128)(2,1)S(1)} %fusion.10), channel_id=1, replica_groups=mesh['dp'=2,'row'=4,'col'=4] {'col'}, dimensions={0}, use_global_device_ids=true | all-gather | bytes 327680 | tf_op jit(solution)/shard_map/all_gather | solution.py:321
  320.0 1.3 fusion.24
  321.6 24.4 %reduce-scatter.21.cloned.1.call-done.upstream_ref = f32[128,512]{1,0:T(8,128)} async-done(((f32[512,512]{1,0:T(8,128)}), f32[128,512]{1,0:T(8,128)}) %reduce-scatter.21.cloned.1.call-update) | async-done | bytes 262160 | tf_op jit(solution)/shard_map/reduce_scatter | solution.py:337
  346.0 10.2 %mixer_backward.1 = (bf16[128,1540]{1,0:T(8,128)(2,1)}, f32[4,256]{1,0:T(4,128)}, f32[4,256]{1,0:T(4,128)}, f32[4,512]{1,0:T(4,128)}, f32[1,256]{1,0:T(1,128)}, /*index=5*/f32[128,4]{1,0:T(8,128)}) custom-call(s32[2,1]{1,0:T(2,128)} %pad_add_fusion.bounds_ref, f32[2]{0:T(128)} %log_ref.3, f32[2]{0:T(128)} %bias_ref.3, ...), custom_call_target="tpu_custom_call" | custom-call | tf_op jit(solution)/shard_map/mixer_backward/pallas_call | solution.py:267
  362.5 31.6 %all-gather.18.cloned.1.call-done = bf16[512,1540]{1,0:T(8,128)(2,1)} async-done(((bf16[128,1540]{1,0:T(8,128)(2,1)}), bf16[512,1540]{1,0:T(8,128)(2,1)}) %all-gather.18.cloned.1.call-update) | async-done | bytes 1576976 | tf_op jit(solution)/shard_map/all_gather | solution.py:325
  394.1 2.9 fusion.25
  397.1 18.6 %all_gather.73 = bf16[512,704]{1,0:T(8,128)(2,1)S(1)} all-gather(bf16[128,704]{1,0:T(8,128)(2,1)S(1)} %get-tuple-element.116), channel_id=1, replica_groups=mesh['dp'=2,'row'=4,'col'=4] {'row'}, dimensions={0}, use_global_device_ids=true | all-gather | bytes 901120 | tf_op jit(solution)/shard_map/all_gather | solution.py:325
  415.7 2.2 convolution_convert_fusion.2
  417.9 1.4 collective-permute-start.9
  419.4 1.2 fusion.21
  422.0 1.4 collective-permute-start.7
  423.5 6.1 %collective-permute-done.9 = bf16[704,256]{1,0:T(8,128)(2,1)} collective-permute-done((bf16[704,256]{1,0:T(8,128)(2,1)}, bf16[704,256]{1,0:T(8,128)(2,1)}, u32[]{:S(2)}, u32[]{:S(2)}) %collective-permute-start.9) | collective-permute-done | bytes 360480 | tf_op jit(solution)/shard_map/ppermute | solution.py:348
  429.6 2.0 convert_add_fusion.2
  431.6 1.1 convolution_convert_fusion.3
  432.7 1.4 collective-permute-start.6
  434.1 3.9 collective-permute-done.8
  437.9 8.0 %collective-permute-done.7 = bf16[256,704]{1,0:T(8,128)(2,1)S(1)} collective-permute-done((bf16[256,704]{1,0:T(8,128)(2,1)S(1)}, bf16[256,704]{1,0:T(8,128)(2,1)S(1)}, u32[]{:S(2)}, u32[]{:S(2)}) %collective-permute-start.7) | collective-permute-done | bytes 360480 | tf_op jit(solution)/shard_map/ppermute | solution.py:348
  445.9 1.1 convert_add_fusion
  447.0 1.1 copy.76
  448.2 1.1 copy.77
  449.3 1.9 convert_add_fusion.3
  451.2 16.8 %all-reduce.3.cloned.1.call-done = f32[34848]{0:T(1024)} async-done(((f32[34848]{0:T(1024)}), f32[34848]{0:T(1024)}) %all-reduce.3.cloned.1.call-update) | async-done | bytes 139408
  467.9 1.0 reshape.120
  471.5 5.3 all-gather.12
  479.1 1.2 collective-permute-start.4
  481.2 1.2 collective-permute-start
  483.2 1.2 collective-permute-start.2
  485.0 1.7 collective-permute-done.1
  486.7 2.8 collective-permute-done
  491.3 3.9 collective-permute-done.3
  495.2 4.4 collective-permute-done.2
  499.7 1.0 copy.74
  500.7 1.0 copy.75
  501.7 1.0 fusion.7
  502.8 9.9 %all-gather.10 = f32[4,1,128]{2,1,0:T(1,128)S(1)} all-gather(f32[1,1,128]{2,1,0:T(1,128)S(1)} %bitcast.56), channel_id=5, replica_groups=mesh['dp'=2,'row'=4,'col'=4] {'row'}, dimensions={0}, use_global_device_ids=true | all-gather | bytes 2560 | tf_op jit(solution)/shard_map/all_gather | solution.py:297
  512.7 8.9 %all-gather.11 = f32[8,1,512]{2,1,0:T(1,128)S(1)} all-gather(f32[1,1,512]{2,1,0:T(1,128)S(1)} %bitcast.47), channel_id=6, replica_groups=mesh['dp'=2,'row'=4,'col'=4] {'dp','col'}, dimensions={0}, use_global_device_ids=true | all-gather | bytes 18432 | tf_op jit(solution)/shard_map/all_gather | solution.py:297
  522.2 1.8 fusion.5
  (118 shorter events, 24.1 us)
Async XLA Ops:
  7.2 122.7 %copy-start = (bf16[704,256]{1,0:T(8,128)(2,1)S(1)}, bf16[704,256]{1,0:T(8,128)(2,1)}, u32[]{:S(2)}) copy-start(bf16[704,256]{1,0:T(8,128)(2,1)} %param.40) | copy-start | bytes 1081348
  7.2 88.6 %reduce-scatter.9.cloned.1.call-start = ((), (), s32[]{:S(2)}) async-start(), calls=%async_computation.8 | async-start | bytes 4259840 | tf_op jit(solution)/shard_map/reduce_scatter | solution.py:337
  32.9 0.7 copy-start.17
  32.9 0.7 copy-start.18
  32.9 89.3 %copy-start.9 = (bf16[512,256]{1,0:T(8,128)(2,1)S(1)}, bf16[512,256]{1,0:T(8,128)(2,1)}, u32[]{:S(2)}) copy-start(bf16[512,256]{1,0:T(8,128)(2,1)} %param.36) | copy-start | bytes 786436
  33.0 90.4 %copy-start.12 = (bf16[128,256]{1,0:T(8,128)(2,1)S(1)}, bf16[128,256]{1,0:T(8,128)(2,1)}, u32[]{:S(2)}) copy-start(bf16[128,256]{1,0:T(8,128)(2,1)} %param.41) | copy-start | bytes 196612
  33.0 112.5 %reduce-scatter.11.cloned.1.call-start = ((), (), s32[]{:S(2)}) async-start(), calls=%async_computation.9 | async-start | bytes 655360 | tf_op jit(solution)/shard_map/reduce_scatter | solution.py:342
  121.4 0.8 copy-start.4
  123.4 59.9 %reduce-scatter.17.cloned.1.call-start = ((), (), s32[]{:S(2)}) async-start(), calls=%async_computation.12 | async-start | bytes 1966080 | tf_op jit(solution)/shard_map/reduce_scatter | solution.py:337
  129.2 0.7 copy-start.8
  129.9 1.6 copy-start.14
  131.5 14.0 %copy-start.6 = (bf16[128,256]{1,0:T(8,128)(2,1)S(1)}, bf16[128,256]{1,0:T(8,128)(2,1)}, u32[]{:S(2)}) copy-start(bf16[128,256]{1,0:T(8,128)(2,1)} %param.22) | copy-start | bytes 196612
  131.5 25.9 %copy-start.15 = (f32[256]{0:T(256)S(1)}, f32[256]{0:T(256)}, u32[]{:S(2)}) copy-start(f32[256]{0:T(256)} %param.37) | copy-start | bytes 3076
  131.5 109.1 %reduce-scatter.13.cloned.1.call-start = ((), (), s32[]{:S(2)}) async-start(), calls=%async_computation.10 | async-start | bytes 3604480 | tf_op jit(solution)/shard_map/reduce_scatter | solution.py:337
  165.5 112.2 %all-gather.16.cloned.1.call-start = ((), (), s32[]{:S(2)}) async-start(), calls=%async_computation.13 | async-start | bytes 1802240 | tf_op jit(solution)/shard_map/all_gather | solution.py:325
  243.0 58.2 %reduce-scatter.19.cloned.1.call-start = ((), (), s32[]{:S(2)}) async-start(), calls=%async_computation.14 | async-start | bytes 655360 | tf_op jit(solution)/shard_map/reduce_scatter | solution.py:342
  280.4 65.6 %reduce-scatter.21.cloned.1.call-start = ((), (), s32[]{:S(2)}) async-start(), calls=%async_computation.15 | async-start | bytes 1310720 | tf_op jit(solution)/shard_map/reduce_scatter | solution.py:337
  320.0 36.2 %copy-start.10 = (bf16[512,256]{1,0:T(8,128)(2,1)}, bf16[512,256]{1,0:T(8,128)(2,1)S(1)}, u32[]{:S(2)}) copy-start(bf16[512,256]{1,0:T(8,128)(2,1)S(1)} %all_gather.78) | copy-start | bytes 786436
  321.3 35.0 %copy-start.19 = (u32[32]{0:T(128)S(1)}, u32[32]{0:T(128)}, u32[]{:S(2)}) copy-start(u32[32]{0:T(128)} %constant.41) | copy-start | bytes 388
  321.4 72.7 %all-gather.18.cloned.1.call-start = ((), (), s32[]{:S(2)}) async-start(), calls=%async_computation.16 | async-start | bytes 2129920 | tf_op jit(solution)/shard_map/all_gather | solution.py:325
  356.2 111.7 %all-reduce.3.cloned.1.call-start = ((), (), s32[]{:S(2)}) async-start(), calls=%async_computation.18 | async-start | bytes 286720
  361.7 0.7 copy-start.13
  362.4 139.3 %reduce-scatter.23.cloned.1.call-start = ((), (), s32[]{:S(2)}) async-start(), calls=%async_computation.17 | async-start | bytes 655360 | tf_op jit(solution)/shard_map/reduce_scatter | solution.py:342
  397.0 125.2 %reduce-scatter.15.cloned.1.call-start = ((), (), s32[]{:S(2)}) async-start(), calls=%async_computation.11 | async-start | bytes 655360 | tf_op jit(solution)/shard_map/reduce_scatter | solution.py:342
  415.7 4.8 copy-start.2
  417.9 11.7 %collective-permute-start.9 = (bf16[704,256]{1,0:T(8,128)(2,1)}, bf16[704,256]{1,0:T(8,128)(2,1)}, u32[]{:S(2)}, u32[]{:S(2)}) collective-permute-start(bf16[704,256]{1,0:T(8,128)(2,1)} %convolution_convert_fusion.2), channel_id=1, source_target_pairs={{0,16},{16,0},{1,17},{17,1},{2,18},{18,2},{3,19},{19,3},{4,20},{20... | collective-permute-start | bytes 1081352 | tf_op jit(solution)/shard_map/ppermute | solution.py:348
  421.2 10.5 %copy-start.5 = (bf16[512,512]{1,0:T(8,128)(2,1)S(1)}, bf16[512,512]{1,0:T(8,128)(2,1)}, u32[]{:S(2)}) copy-start(bf16[512,512]{1,0:T(8,128)(2,1)} %copy-done.4) | copy-start | bytes 1572868
  421.2 10.5 %copy-start.11 = (bf16[512,256]{1,0:T(8,128)(2,1)S(1)}, bf16[512,256]{1,0:T(8,128)(2,1)}, u32[]{:S(2)}) copy-start(bf16[512,256]{1,0:T(8,128)(2,1)} %copy-done.10) | copy-start | bytes 786436
  421.4 16.5 %collective-permute-start.8 = (bf16[256,704]{1,0:T(8,128)(2,1)S(1)}, bf16[256,704]{1,0:T(8,128)(2,1)S(1)}, u32[]{:S(2)}, u32[]{:S(2)}) collective-permute-start(bf16[256,704]{1,0:T(8,128)(2,1)S(1)} %get-tuple-element.119), channel_id=1, source_target_pairs={{0,16},{16,0},{1,17},{17,1},{2,18},{18,2},{3,19},{19,3},{4,20},{20... | collective-permute-start | bytes 1081352 | tf_op jit(solution)/shard_map/ppermute | solution.py:348
  422.0 23.9 %collective-permute-start.7 = (bf16[256,704]{1,0:T(8,128)(2,1)S(1)}, bf16[256,704]{1,0:T(8,128)(2,1)S(1)}, u32[]{:S(2)}, u32[]{:S(2)}) collective-permute-start(bf16[256,704]{1,0:T(8,128)(2,1)S(1)} %get-tuple-element.120), channel_id=1, source_target_pairs={{0,16},{16,0},{1,17},{17,1},{2,18},{18,2},{3,19},{19,3},{4,20},{20... | collective-permute-start | bytes 1081352 | tf_op jit(solution)/shard_map/ppermute | solution.py:348
  432.7 16.6 %collective-permute-start.6 = (bf16[512,256]{1,0:T(8,128)(2,1)}, bf16[512,256]{1,0:T(8,128)(2,1)}, u32[]{:S(2)}, u32[]{:S(2)}) collective-permute-start(bf16[512,256]{1,0:T(8,128)(2,1)} %convolution_convert_fusion.3), channel_id=1, source_target_pairs={{0,16},{16,0},{1,17},{17,1},{2,18},{18,2},{3,19},{19,3},{4,20},{20... | collective-permute-start | bytes 786440 | tf_op jit(solution)/shard_map/ppermute | solution.py:348
  447.0 1.1 copy-start.3
  448.1 29.2 %copy-start.1 = (bf16[512,1540]{1,0:T(8,128)(2,1)S(1)}, bf16[512,1540]{1,0:T(8,128)(2,1)}, u32[]{:S(2)}) copy-start(bf16[512,1540]{1,0:T(8,128)(2,1)} %all-gather.18.cloned.1.call-done) | copy-start | bytes 4730884
  478.2 5.0 collective-permute-start.5
  479.1 5.4 %collective-permute-start.4 = (bf16[256,2]{0,1:T(2,128)(2,1)S(1)}, bf16[256,2]{0,1:T(2,128)(2,1)S(1)}, u32[]{:S(2)}, u32[]{:S(2)}) collective-permute-start(bf16[256,2]{0,1:T(2,128)(2,1)S(1)} %get-tuple-element.107), channel_id=1, source_target_pairs={{0,16},{16,0},{1,17},{17,1},{2,18},{18,2},{3,19},{19,3},{4,20},{20... | collective-permute-start | bytes 3080 | tf_op jit(solution)/shard_map/ppermute | solution.py:348
  480.3 6.4 %collective-permute-start.1 = (bf16[256,256]{0,1:T(8,128)(2,1)S(1)}, bf16[256,256]{0,1:T(8,128)(2,1)S(1)}, u32[]{:S(2)}, u32[]{:S(2)}) collective-permute-start(bf16[256,256]{0,1:T(8,128)(2,1)S(1)} %get-tuple-element.114), channel_id=1, source_target_pairs={{0,16},{16,0},{1,17},{17,1},{2,18},{18,2},{3,19},{19,3},{4,20},{20... | collective-permute-start | bytes 393224 | tf_op jit(solution)/shard_map/ppermute | solution.py:348
  481.2 8.4 %collective-permute-start = (bf16[256,256]{0,1:T(8,128)(2,1)S(1)}, bf16[256,256]{0,1:T(8,128)(2,1)S(1)}, u32[]{:S(2)}, u32[]{:S(2)}) collective-permute-start(bf16[256,256]{0,1:T(8,128)(2,1)S(1)} %get-tuple-element.115), channel_id=1, source_target_pairs={{0,16},{16,0},{1,17},{17,1},{2,18},{18,2},{3,19},{19,3},{4,20},{20... | collective-permute-start | bytes 393224 | tf_op jit(solution)/shard_map/ppermute | solution.py:348
  482.4 12.8 %collective-permute-start.3 = (bf16[256,512]{0,1:T(8,128)(2,1)S(1)}, bf16[256,512]{0,1:T(8,128)(2,1)S(1)}, u32[]{:S(2)}, u32[]{:S(2)}) collective-permute-start(bf16[256,512]{0,1:T(8,128)(2,1)S(1)} %get-tuple-element.110), channel_id=1, source_target_pairs={{0,16},{16,0},{1,17},{17,1},{2,18},{18,2},{3,19},{19,3},{4,20},{20... | collective-permute-start | bytes 786440 | tf_op jit(solution)/shard_map/ppermute | solution.py:348
  483.2 16.4 %collective-permute-start.2 = (bf16[256,512]{0,1:T(8,128)(2,1)S(1)}, bf16[256,512]{0,1:T(8,128)(2,1)S(1)}, u32[]{:S(2)}, u32[]{:S(2)}) collective-permute-start(bf16[256,512]{0,1:T(8,128)(2,1)S(1)} %get-tuple-element.111), channel_id=1, source_target_pairs={{0,16},{16,0},{1,17},{17,1},{2,18},{18,2},{3,19},{19,3},{4,20},{20... | collective-permute-start | bytes 786440 | tf_op jit(solution)/shard_map/ppermute | solution.py:348
  491.3 10.4 %copy-start.16 = (f32[256]{0:T(256)S(1)}, f32[256]{0:T(256)}, u32[]{:S(2)}) copy-start(f32[256]{0:T(256)} %param.23) | copy-start | bytes 3076
  499.7 22.5 %copy-start.7 = (f32[128,256]{1,0:T(8,128)S(1)}, f32[128,256]{1,0:T(8,128)}, u32[]{:S(2)}) copy-start(f32[128,256]{1,0:T(8,128)} %reduce-scatter.19.cloned.1.call-done) | copy-start | bytes 393220
Sparse Core Ops, SparseCore 0:
  33.1 62.6 reduce-scatter.8
  123.5 21.9 reduce-scatter.10
  147.8 35.4 reduce-scatter.16
  185.4 55.1 reduce-scatter.12
  243.1 34.4 all-gather.15
  280.6 20.6 reduce-scatter.18
  321.5 24.5 reduce-scatter.20
  356.4 37.6 all-gather.17
  398.0 69.8 all-reduce.2
  470.3 20.7 reduce-scatter.22
  493.5 21.6 reduce-scatter.14
